TPU v7x, 512 devices: a whole 4x8x8 slice. The times are simulated.
512 devices in a mesh: ab: 32 (over z, x), cd: 16 (over y, core).
Axes of the slice: x: 4, y: 8, z: 8, core: 2. Of those that a mesh axis runs over, the one named last changes fastest.
Arguments:
- amplitudes: float32 [512, 8192], P('ab', 'cd'), may hold values from -6 to 6
- integrals: float32 [65536, 8192], P('ab', 'cd'), may hold values from -0.125 to 0.125
- ij_pairs: int32 [512, 2], P('cd'), may hold values from 0 to 127
- ab_pairs: int32 [65536, 2], P('ab'), may hold values from 0 to 1535
- eps_occ: float32 [128], replicated, may hold values from -1.5 to -0.3
- eps_vir: float32 [1536], replicated, may hold values from 0.1 to 2.5
Outputs:
- ladder: float32 [512, 65536], P('cd', 'ab')
- update: float32 [512, 65536], P('cd', 'ab')
All inputs are finite; a program needn't handle non-finite values.
Results may differ from a plain program's by a relative error of at most 0.00015.
Values sent between devices are 32-bit elements; how exact they have to be, the bound alone decides.
A program may use at most 64 MiB of HBM per device.

v0:
```python
import jax
import jax.numpy as jnp
from jax import lax
from jax.sharding import PartitionSpec as P


def lookup_energy(indices, energies):
    positions = lax.broadcasted_iota(jnp.int32, (indices.shape[0], energies.shape[0]), 1)
    picked = jnp.where(indices[:, None] == positions, energies[None, :], jnp.float32(0.0))
    return jnp.sum(picked, axis=1)


def contract_rows(row_block, col_block):
    return lax.dot_general(
        row_block,
        col_block,
        (((1,), (1,)), ((), ())),
        precision=lax.Precision.HIGHEST,
        preferred_element_type=jnp.float32,
    )


def on_device(amplitudes, integrals, ij_pairs, ab_pairs, eps_occ, eps_vir):
    partial_value = contract_rows(lax.all_gather(amplitudes, "ab", axis=0, tiled=True), integrals)
    ladder = lax.psum_scatter(partial_value, "cd", scatter_dimension=0, tiled=True)
    first_occ = lookup_energy(ij_pairs[:, 0], eps_occ)[:, None]
    second_occ = lookup_energy(ij_pairs[:, 1], eps_occ)[:, None]
    first_vir = lookup_energy(ab_pairs[:, 0], eps_vir)[None, :]
    second_vir = lookup_energy(ab_pairs[:, 1], eps_vir)[None, :]
    denominator = first_occ + second_occ - first_vir - second_vir
    update = ladder / denominator
    return (ladder, update)


def solution(mesh):
    in_specs = (P("ab", "cd"), P("ab", "cd"), P("cd", None), P("ab", None), P(), P())
    out_specs = (P("cd", "ab"), P("cd", "ab"))
    return jax.shard_map(
        on_device, mesh=mesh, in_specs=in_specs, out_specs=out_specs, check_vma=False
    )
```

profile of v0, /device:TPU:27, one launch (start us, length us, event | category | flops | bytes accessed | tf_op | source)
XLA Modules:
  0.0 179.7 jit_solution(8097404686899207612)
XLA Ops:
  7.2 0.0 all-gather.2.cloned.1.call-start
  7.2 0.7 all-gather.2.cloned.1.call-update
  7.9 0.0 reduce-scatter.2.cloned.1.call-start
  7.9 84.6 %all-gather.2.cloned.1.call-done = f32[512,512]{1,0:T(8,128)} async-done(((f32[16,512]{1,0:T(8,128)}), f32[512,512]{1,0:T(8,128)}) %all-gather.2.cloned.1.call-update) | async-done | bytes 1048592 | tf_op jit(solution)/shard_map/all_gather | solution.py:24
  92.5 10.4 %fusion.1 = f32[512,2048]{1,0:T(8,128)} fusion(f32[512,512]{1,0:T(8,128)} %all-gather.2.cloned.1.call-done, f32[2048,512]{1,0:T(8,128)} %param.7), kind=kOutput, calls=%fused_computation.12 | convolution fusion | flops 6442450944 | bytes 9437184 | tf_op jit(solution)/shard_map/dot_general | solution.py:14
  102.9 0.0 copy-start.1
  102.9 0.0 copy-start.2
  102.9 0.0 copy-start
  102.9 0.0 copy-start.3
  102.9 0.0 reduce-scatter.2.cloned.1.call-update
  102.9 0.6 copy-done.1
  103.5 0.0 copy-done.2
  103.5 0.2 select_reduce_fusion.2
  103.7 0.0 copy-done
  103.8 0.0 copy-done.3
  103.8 3.9 %select_reduce_fusion.1 = (f32[2048]{0:T(1024)S(1)}, f32[2048]{0:T(1024)S(1)}) fusion(f32[1536]{0:T(1024)S(1)} %copy-done.3, s32[2048]{0:T(1024)S(1)} %bitcast.9, s32[2048]{0:T(1024)S(1)} %bitcast.8), kind=kLoop, calls=%fused_computation.2 | loop fusion | flops 18870272 | bytes 38912 | tf_op jit(solution)/shard_map/reduce_sum | solution.py:10
  107.7 63.4 %reduce-scatter.2.cloned.1.call-done = f32[32,2048]{1,0:T(8,128)} async-done(((f32[512,2048]{1,0:T(8,128)}), f32[32,2048]{1,0:T(8,128)}) %reduce-scatter.2.cloned.1.call-update) | async-done | bytes 262160 | tf_op jit(solution)/shard_map/reduce_scatter | solution.py:25
  171.1 1.8 subtract_divide_fusion
  (3 shorter events, 0.0 us)
Async XLA Ops:
  7.2 85.3 %all-gather.2.cloned.1.call-start = ((), (), s32[]{:S(2)}) async-start(), calls=%async_computation.1 | async-start | bytes 1081344 | tf_op jit(solution)/shard_map/all_gather | solution.py:24
  7.9 163.2 %reduce-scatter.2.cloned.1.call-start = ((), (), s32[]{:S(2)}) async-start(), calls=%async_computation.2 | async-start | bytes 4456448 | tf_op jit(solution)/shard_map/reduce_scatter | solution.py:25
  102.9 0.7 copy-start.1
  102.9 0.7 copy-start.2
  102.9 0.9 copy-start
  102.9 0.9 copy-start.3
Sparse Core Ops, SparseCore 0:
  11.2 81.2 all-gather.1
  103.0 67.9 reduce-scatter.1
where the time goes:
time: 180 us
  waiting for transfers between devices  149 us (83%)
  between operations  14.1 us (8%)
  matrix products  10.4 us (6%)
  other arithmetic  5.86 us (3%)
    all_gather x1, waiting for transfers between devices, on_device(): lax.all_gather(amplitudes, 'ab', axis=0, tiled=True)  84.6 us
    reduce_scatter x1, waiting for transfers between devices, on_device(): lax.psum_scatter(partial_value, 'cd', scatter_dimension=0, tiled=True)  63.4 us
    dot_general x1, matrix products, contract_rows(): lax.dot_general(row_block, col_block, (((1,), (1,)), ((), ())), precision...  10.4 us
    reduce_sum x2, other arithmetic, lookup_energy(): return jnp.sum(picked, axis=1)  4.09 us
  transfers between devices with their start and end apart: 2, of which 2 were waited for; matrix products, arithmetic and copies ran while one was open for 2% of the time, Pallas kernels for 0%

commit v1 on v0

--- a/solution.py
+++ b/solution.py
@@ -2,6 +2,14 @@
 import jax.numpy as jnp
 from jax import lax
 from jax.sharding import PartitionSpec as P
+
+
+def gather_from_all(array, axis, dim):
+    size = lax.axis_size(axis)
+    repeats = [size if d == dim else 1 for d in range(array.ndim)]
+    return lax.all_to_all(
+        jnp.tile(array, repeats), axis, split_axis=dim, concat_axis=dim, tiled=True
+    )
 
 
 def lookup_energy(indices, energies):
@@ -21,7 +29,7 @@
 
 
 def on_device(amplitudes, integrals, ij_pairs, ab_pairs, eps_occ, eps_vir):
-    partial_value = contract_rows(lax.all_gather(amplitudes, "ab", axis=0, tiled=True), integrals)
+    partial_value = contract_rows(gather_from_all(amplitudes, "ab", 0), integrals)
     ladder = lax.psum_scatter(partial_value, "cd", scatter_dimension=0, tiled=True)
     first_occ = lookup_energy(ij_pairs[:, 0], eps_occ)[:, None]
     second_occ = lookup_energy(ij_pairs[:, 1], eps_occ)[:, None]

time: 180 us -> 131 us (0.73)
  the two profiles are of different devices: /device:TPU:27 before, /device:TPU:29 now
where the time goes in v1:
time: 131 us; the launch traced here: 130 us
  waiting for transfers between devices  59 us (45%)
  blocking collectives  39.6 us (30%)
  between operations  14.1 us (11%)
  matrix products  10.1 us (8%)
  other arithmetic  5.86 us (4%)
  local copies, waits for them, and re-layouts  1.54 us (1%)
    reduce_scatter x1, waiting for transfers between devices, on_device(): lax.psum_scatter(partial_value, 'cd', scatter_dimension=0, tiled=True)  58.9 us
    all_to_all x1, blocking collectives, gather_from_all(): lax.all_to_all(jnp.tile(array, repeats), axis, split_axis=dim, concat_axi...  39.6 us
    dot_general x1, matrix products, contract_rows(): lax.dot_general(row_block, col_block, (((1,), (1,)), ((), ())), precision...  10.1 us
    reduce_sum x2, other arithmetic, lookup_energy(): return jnp.sum(picked, axis=1)  4.09 us
  transfers between devices with their start and end apart: 1, of which 1 were waited for; matrix products, arithmetic and copies ran while one was open for 3% of the time, Pallas kernels for 0%

profile of v1, /device:TPU:29, one launch (start us, length us, event | category | flops | bytes accessed | tf_op | source)
XLA Modules:
  0.0 130.2 jit_solution(6418490993698102634)
XLA Ops:
  7.2 0.0 reduce-scatter.2.cloned.1.call-start
  7.2 0.9 tile.2
  8.1 39.6 %all_to_all.9 = f32[32,16,512]{2,1,0:T(8,128)S(1)} all-to-all(f32[32,16,512]{2,1,0:T(8,128)S(1)} %tile.2), channel_id=1, replica_groups=mesh['ab'=32,'cd'=16] {'ab'}, dimensions={0} | all-to-all | bytes 2097152 | tf_op jit(solution)/shard_map/all_to_all | solution.py:10
  47.7 10.1 %fusion.1 = f32[512,2048]{1,0:T(8,128)} fusion(f32[512,512]{1,0:T(8,128)S(1)} %bitcast.9, f32[2048,512]{1,0:T(8,128)} %param.7), kind=kOutput, calls=%fused_computation.12 | convolution fusion | flops 6442450944 | bytes 9437184 | tf_op jit(solution)/shard_map/dot_general | solution.py:22
  57.8 0.0 copy-start.1
  57.8 0.0 copy-start.2
  57.8 0.0 copy-start
  57.8 0.0 copy-start.3
  57.9 0.0 reduce-scatter.2.cloned.1.call-update
  57.9 0.6 copy-done.1
  58.5 0.0 copy-done.2
  58.5 0.2 select_reduce_fusion.2
  58.7 0.0 copy-done
  58.8 0.0 copy-done.3
  58.8 3.9 %select_reduce_fusion.1 = (f32[2048]{0:T(1024)S(1)}, f32[2048]{0:T(1024)S(1)}) fusion(f32[1536]{0:T(1024)S(1)} %copy-done.3, s32[2048]{0:T(1024)S(1)} %bitcast.11, s32[2048]{0:T(1024)S(1)} %bitcast.10), kind=kLoop, calls=%fused_computation.2 | loop fusion | flops 18870272 | bytes 38912 | tf_op jit(solution)/shard_map/reduce_sum | solution.py:18
  62.7 58.9 %reduce-scatter.2.cloned.1.call-done = f32[32,2048]{1,0:T(8,128)} async-done(((f32[512,2048]{1,0:T(8,128)}), f32[32,2048]{1,0:T(8,128)}) %reduce-scatter.2.cloned.1.call-update) | async-done | bytes 262160 | tf_op jit(solution)/shard_map/reduce_scatter | solution.py:33
  121.6 1.8 %subtract_divide_fusion = f32[32,2048]{1,0:T(8,128)} fusion(f32[32,2048]{1,0:T(8,128)} %reduce-scatter.2.cloned.1.call-done, f32[2048]{0:T(1024)S(1)} %get-tuple-element.3, f32[2048]{0:T(1024)S(1)} %get-tuple-element.2, f32[32]{0:T(128)S(1)} %add.10), kind=kLoop, calls=%fused_computation.4 | loop fusion | flops 196608 | bytes 540800 | tf_op jit(solution)/shard_map/div | solution.py:39
  (3 shorter events, 0.0 us)
Async XLA Ops:
  7.2 114.5 %reduce-scatter.2.cloned.1.call-start = ((), (), s32[]{:S(2)}) async-start(), calls=%async_computation.2 | async-start | bytes 4456448 | tf_op jit(solution)/shard_map/reduce_scatter | solution.py:33
  57.8 0.7 copy-start.1
  57.8 0.7 copy-start.2
  57.8 0.9 copy-start
  57.8 0.9 copy-start.3
Sparse Core Ops, SparseCore 0:
  58.0 63.5 reduce-scatter.1
